TPU v7x, 128 devices: a whole 4x4x4 slice. The times are simulated.
128 devices in a mesh: req: 16 (over y, x), seq: 8 (over z, core).
Axes of the slice: x: 4, y: 4, z: 4, core: 2. Of those that a mesh axis runs over, the one named last changes fastest.
Arguments:
- qkv_proj: bfloat16 [16, 1024, 4096], P('req', 'seq'), may hold values from -6 to 6
- gate_proj: bfloat16 [16, 1024, 2048], P('req', 'seq'), may hold values from -6 to 6
- residual: bfloat16 [16, 1024, 2048], P('req', 'seq'), may hold values from -6 to 6
- log_decay: float32 [16, 1024, 8], P('req', 'seq'), may hold values from -1 to 0, as said below
- beta_logit: bfloat16 [16, 1024, 8], P('req', 'seq'), may hold values from -6 to 6
- lengths: int32 [16], replicated, may hold values from 1 to 1024, 8192 in all
- slot_request: int32 [16], replicated, may hold values from 0 to 15, each once
- conv_weight: float32 [4, 4096], replicated, may hold values from -3 to 3
- norm_gain: float32 [256], replicated, may hold values from 0.1 to 1.9
- out_weight: bfloat16 [2048, 2048], P(('req', 'seq')), may hold values from -0.125 to 0.125
- mlp_gain: float32 [2048], replicated, may hold values from 0.1 to 1.9
- w_gate: bfloat16 [2048, 5632], P('req', 'seq'), may hold values from -0.125 to 0.125
- w_up: bfloat16 [2048, 5632], P('req', 'seq'), may hold values from -0.125 to 0.125
- w_down: bfloat16 [5632, 2048], P('seq', 'req'), may hold values from -0.078125 to 0.078125
Outputs:
- hidden_out: bfloat16 [16, 1024, 2048], P('req', 'seq')
- final_state: float32 [16, 8, 128, 256], P('req', 'seq')
- conv_edge: bfloat16 [16, 3, 4096], P('req', None, 'seq')
Inputs may be any that keep to these rules, and one draw needn't show every extreme that they name: Slot s of the req axis holds request slot_request[s]. The 16 lengths sum to 8192, and the longest is exactly 1024. `log_decay`: every entry is negative.
All inputs are finite; a program needn't handle non-finite values.
Results may differ from a plain program's by a relative error of at most 0.014.
Values may be sent and summed in bfloat16 or wider, within the bound.
A program may use at most 128 MiB of HBM per device.

v0:
```python
import jax
import jax.numpy as jnp
from jax import lax
from jax.sharding import PartitionSpec as P

LOCAL_HEADS = 8
DK = 128
DV = 256
CONV = 4
BLOCK = 64
HK = 1024
EPS_NORM = 1e-05
EPS_UNIT = 1e-06
HIGHEST = lax.Precision.HIGHEST


def shifted(value, axis, steps):
    count = lax.axis_size(axis)
    initial, last = (max(0, -steps), min(count, count - steps))
    return lax.ppermute(value, axis, [(source, source + steps) for source in range(initial, last)])


def unit_norm(vector):
    return vector * lax.rsqrt(jnp.sum(vector * vector, axis=-1, keepdims=True) + EPS_UNIT)


def to_blocks(tensor, block_len):
    length = tensor.shape[0]
    grouped = tensor.reshape((length // block_len, block_len) + tensor.shape[1:])
    return jnp.moveaxis(grouped, 2, 0)


def block_tables(query_vec, key_vecs, beta_gate, decay_log, block_len):
    query_b = to_blocks(query_vec, block_len)
    keys_b = to_blocks(key_vecs, block_len)
    beta_b = to_blocks(beta_gate, block_len)
    cumulative = jnp.cumsum(to_blocks(decay_log, block_len), axis=-1)
    spread = cumulative[..., :, None] - cumulative[..., None, :]
    lower_full = jnp.tril(jnp.ones((block_len, block_len), jnp.float32))
    lower_strict = jnp.tril(jnp.ones((block_len, block_len), jnp.float32), -1)
    within = jnp.exp(jnp.where(lower_full > 0, spread, 0.0)) * lower_full
    key_inner = jnp.einsum("hnik,hnjk->hnij", keys_b, keys_b, precision=HIGHEST)
    couple = beta_b[..., :, None] * within * lower_strict * key_inner
    identity = jnp.broadcast_to(jnp.eye(block_len, dtype=jnp.float32), couple.shape)
    inverse = lax.linalg.triangular_solve(
        identity + couple, identity, left_side=True, lower=True, unit_diagonal=True
    )
    growth = jnp.exp(cumulative)
    weighted_keys = jnp.einsum(
        "hnij,hnjk->hnik", inverse, (beta_b * growth)[..., None] * keys_b, precision=HIGHEST
    )
    query_keys = jnp.einsum("hnik,hnjk->hnij", query_b, keys_b, precision=HIGHEST) * within
    grown_query = growth[..., None] * query_b
    keys_to_end = jnp.exp(cumulative[..., -1:] - cumulative)[..., None] * keys_b
    end_growth = growth[..., -1]
    return (inverse, beta_b, (weighted_keys, query_keys, grown_query, keys_to_end, end_growth))


def solve_values(inverse, beta_b, values_b):
    return jnp.einsum("hnij,hnjx->hnix", inverse, beta_b[..., None] * values_b, precision=HIGHEST)


def run_blocks(initial, solved, tables):
    weighted_keys, query_keys, grown_query, keys_to_end, end_growth = tables
    sequence = tuple(
        (
            jnp.moveaxis(tensor, 1, 0)
            for tensor in (solved, weighted_keys, query_keys, grown_query, keys_to_end, end_growth)
        )
    )

    def advance(running, inputs_now):
        solved_now, weighted_now, inner_now, query_now, keys_now, growth_now = inputs_now
        corrected = solved_now - jnp.einsum(
            "hck,hkx->hcx", weighted_now, running, precision=HIGHEST
        )
        output_now = jnp.einsum("hck,hkx->hcx", query_now, running, precision=HIGHEST) + jnp.einsum(
            "hcd,hdx->hcx", inner_now, corrected, precision=HIGHEST
        )
        running = growth_now[:, None, None] * running + jnp.einsum(
            "hck,hcx->hkx", keys_now, corrected, precision=HIGHEST
        )
        return (running, output_now)

    return lax.scan(advance, initial, sequence)


def local(
    qkv_proj,
    gate_proj,
    residual,
    log_decay,
    beta_logit,
    lengths,
    slot_request,
    conv_weight,
    norm_gain,
    out_weight,
    mlp_gain,
    w_gate,
    w_up,
    w_down,
):
    seq_index = lax.axis_index("seq")
    req_index = lax.axis_index("req")
    seq_size = lax.axis_size("seq")
    piece_len = qkv_proj.shape[1]
    channels = qkv_proj.shape[2]
    request_ids = jnp.arange(slot_request.shape[0], dtype=jnp.int32)
    request = jnp.sum(jnp.where(request_ids == req_index, slot_request, 0))
    length = jnp.sum(jnp.where(request_ids == request, lengths, 0))
    position = seq_index * piece_len + jnp.arange(piece_len, dtype=jnp.int32)
    live_mask = position < length
    tokens = qkv_proj[0]
    rim_rows = shifted(tokens[piece_len - (CONV - 1) :], "seq", 1)
    extended = jnp.concatenate([rim_rows, tokens], axis=0)
    convolved = jnp.zeros((piece_len, channels), jnp.float32)
    for offset in range(CONV):
        convolved = convolved + conv_weight[offset] * extended[offset : offset + piece_len].astype(
            jnp.float32
        )
    activated = jax.nn.silu(convolved)
    query_vec = unit_norm(activated[:, :HK].reshape(piece_len, LOCAL_HEADS, DK)) * DK ** (-0.5)
    key_vecs = unit_norm(activated[:, HK : 2 * HK].reshape(piece_len, LOCAL_HEADS, DK))
    values = activated[:, 2 * HK :].reshape(piece_len, LOCAL_HEADS, DV)
    beta_gate = jax.nn.sigmoid(beta_logit[0].astype(jnp.float32)) * live_mask[:, None]
    decay_log = jnp.where(live_mask[:, None], log_decay[0], 0.0)
    inverse, beta_b, tables = block_tables(query_vec, key_vecs, beta_gate, decay_log, BLOCK)
    values_b = to_blocks(values, BLOCK)
    solved = solve_values(inverse, beta_b, values_b)
    zero_state = jnp.zeros((LOCAL_HEADS, DK, DV), jnp.float32)
    incoming = zero_state
    for section_index in range(seq_size - 1):
        ending, discarded = run_blocks(incoming, solved, tables)
        incoming = shifted(ending.astype(jnp.bfloat16), "seq", 1).astype(ending.dtype)
    ending, outputs = run_blocks(incoming, solved, tables)
    outputs = jnp.moveaxis(outputs, 1, 2).reshape(piece_len, LOCAL_HEADS, DV)
    is_last = seq_index == seq_size - 1
    state_term = jnp.where(is_last, ending, 0.0)
    targets = length - (CONV - 1) + jnp.arange(CONV - 1, dtype=jnp.int32)
    select = (position[None, :] == targets[:, None]).astype(jnp.bfloat16)
    edge_term = jnp.dot(select, tokens, preferred_element_type=jnp.float32)
    state_part, edge_part = (
        lax.psum_scatter(
            state_term.astype(jnp.bfloat16), "seq", scatter_dimension=0, tiled=True
        ).astype(jnp.float32),
        lax.psum_scatter(
            edge_term.astype(jnp.bfloat16), "seq", scatter_dimension=1, tiled=True
        ).astype(jnp.float32),
    )
    gate_values = gate_proj[0].astype(jnp.float32).reshape(piece_len, LOCAL_HEADS, DV)
    scaled = outputs * lax.rsqrt(jnp.mean(outputs * outputs, axis=-1, keepdims=True) + EPS_NORM)
    mixed_heads = (
        (scaled * norm_gain * jax.nn.silu(gate_values))
        .reshape(piece_len, LOCAL_HEADS * DV)
        .astype(jnp.bfloat16)
    )
    attended = jnp.dot(
        mixed_heads,
        lax.all_gather(out_weight, ("req", "seq"), axis=0, tiled=True),
        preferred_element_type=jnp.float32,
    )
    hidden_state = (residual[0].astype(jnp.float32) + attended).astype(jnp.bfloat16)
    stream = hidden_state.astype(jnp.float32)
    normed = (
        stream * lax.rsqrt(jnp.mean(stream * stream, axis=-1, keepdims=True) + EPS_NORM) * mlp_gain
    ).astype(jnp.bfloat16)
    gate_full, up_full = (
        lax.all_gather(w_gate, "req", axis=0, tiled=True),
        lax.all_gather(w_up, "req", axis=0, tiled=True),
    )
    down_full = lax.all_gather(w_down, "req", axis=1, tiled=True)
    shard_rows = lax.all_gather(normed, "seq", axis=0, tiled=True)
    gate_part = jnp.dot(shard_rows, gate_full, preferred_element_type=jnp.float32)
    upward = jnp.dot(shard_rows, up_full, preferred_element_type=jnp.float32)
    inner_units = (jax.nn.silu(gate_part) * upward).astype(jnp.bfloat16)
    summed = lax.psum_scatter(
        jnp.dot(inner_units, down_full, preferred_element_type=jnp.float32).astype(jnp.bfloat16),
        "seq",
        scatter_dimension=0,
        tiled=True,
    ).astype(jnp.float32)
    combined = stream + summed
    hidden_out = jnp.where(live_mask[:, None], combined, 0.0).astype(jnp.bfloat16)
    return (hidden_out[None], state_part[None], edge_part.astype(jnp.bfloat16)[None])


def solution(mesh):
    return jax.shard_map(
        local,
        mesh=mesh,
        in_specs=(
            P("req", "seq", None),
            P("req", "seq", None),
            P("req", "seq", None),
            P("req", "seq", None),
            P("req", "seq", None),
            P(),
            P(),
            P(),
            P(),
            P(("req", "seq"), None),
            P(),
            P("req", "seq"),
            P("req", "seq"),
            P("seq", "req"),
        ),
        out_specs=(P("req", "seq", None), P("req", "seq", None, None), P("req", None, "seq")),
        check_vma=False,
    )
```

profile of v0, /device:TPU:0, one launch (start us, length us, event | category | flops | bytes accessed | tf_op | source)
XLA Modules:
  0.0 511.9 jit_solution(8159952312244182873)
XLA Ops:
  8.1 1.3 collective-permute-start
  11.0 1.3 fusion.105
  12.3 1.9 fusion.106
  17.2 3.4 divide_multiply_fusion
  20.6 1.4 multiply_bitcast_fusion
  22.8 1.1 broadcast_multiply_fusion
  23.9 1.8 fusion.72
  25.7 80.0 %custom-call.3 = f32[8,2,1,64,64]{3,4,2,1,0:T(8,128)} custom-call(f32[8,2,1,64,64]{4,3,2,1,0:T(8,128)} %fusion.72), custom_call_target="InvertDiagBlocksLowerTriangular" | custom-call | tf_op jit(solution)/shard_map/triangular_solve | solution.py:45
  105.7 2.0 fusion.85
  107.8 1.7 convolution_bitcast_fusion.2
  109.9 1.3 convolution_bitcast_fusion
  111.8 4.1 while.90
  112.5 1.3 convolution_add_fusion.25
  114.6 1.3 convolution_add_fusion.25
  116.8 5.9 %collective-permute-start.1 = (bf16[8,128,256]{2,1,0:T(8,128)(2,1)}, bf16[8,128,256]{2,1,0:T(8,128)(2,1)}, u32[]{:S(2)}, u32[]{:S(2)}) collective-permute-start(bf16[8,128,256]{2,1,0:T(8,128)(2,1)} %convert_element_type.129), channel_id=1, source_target_pairs={{0,1},{1,2},{2,3},{3,4},{4,5},{5,6},{6,7},{8,9},{9,10},{10,11},{11... | collective-permute-start | bytes 1572872 | tf_op jit(solution)/shard_map/ppermute | solution.py:20
  124.5 4.2 while.83
  125.3 1.3 convolution_add_fusion.18
  127.4 1.3 convolution_add_fusion.18
  129.6 7.3 %collective-permute-start.2 = (bf16[8,128,256]{2,1,0:T(8,128)(2,1)}, bf16[8,128,256]{2,1,0:T(8,128)(2,1)}, u32[]{:S(2)}, u32[]{:S(2)}) collective-permute-start(bf16[8,128,256]{2,1,0:T(8,128)(2,1)} %convert_element_type.131), channel_id=1, source_target_pairs={{0,1},{1,2},{2,3},{3,4},{4,5},{5,6},{6,7},{8,9},{9,10},{10,11},{11... | collective-permute-start | bytes 1572872 | tf_op jit(solution)/shard_map/ppermute | solution.py:20
  139.1 4.2 while.84
  139.8 1.3 convolution_add_fusion.19
  141.9 1.3 convolution_add_fusion.19
  144.2 9.7 %collective-permute-start.3 = (bf16[8,128,256]{2,1,0:T(8,128)(2,1)}, bf16[8,128,256]{2,1,0:T(8,128)(2,1)}, u32[]{:S(2)}, u32[]{:S(2)}) collective-permute-start(bf16[8,128,256]{2,1,0:T(8,128)(2,1)} %convert_element_type.133), channel_id=1, source_target_pairs={{0,1},{1,2},{2,3},{3,4},{4,5},{5,6},{6,7},{8,9},{9,10},{10,11},{11... | collective-permute-start | bytes 1572872 | tf_op jit(solution)/shard_map/ppermute | solution.py:20
  156.1 4.2 while.85
  156.9 1.3 convolution_add_fusion.20
  159.0 1.3 convolution_add_fusion.20
  161.2 9.7 %collective-permute-start.4 = (bf16[8,128,256]{2,1,0:T(8,128)(2,1)}, bf16[8,128,256]{2,1,0:T(8,128)(2,1)}, u32[]{:S(2)}, u32[]{:S(2)}) collective-permute-start(bf16[8,128,256]{2,1,0:T(8,128)(2,1)} %convert_element_type.135), channel_id=1, source_target_pairs={{0,1},{1,2},{2,3},{3,4},{4,5},{5,6},{6,7},{8,9},{9,10},{10,11},{11... | collective-permute-start | bytes 1572872 | tf_op jit(solution)/shard_map/ppermute | solution.py:20
  173.2 4.2 while.86
  173.9 1.3 convolution_add_fusion.21
  176.0 1.3 convolution_add_fusion.21
  178.3 9.7 %collective-permute-start.5 = (bf16[8,128,256]{2,1,0:T(8,128)(2,1)}, bf16[8,128,256]{2,1,0:T(8,128)(2,1)}, u32[]{:S(2)}, u32[]{:S(2)}) collective-permute-start(bf16[8,128,256]{2,1,0:T(8,128)(2,1)} %convert_element_type.137), channel_id=1, source_target_pairs={{0,1},{1,2},{2,3},{3,4},{4,5},{5,6},{6,7},{8,9},{9,10},{10,11},{11... | collective-permute-start | bytes 1572872 | tf_op jit(solution)/shard_map/ppermute | solution.py:20
  190.2 4.2 while.87
  191.0 1.3 convolution_add_fusion.22
  193.0 1.3 convolution_add_fusion.22
  195.2 9.7 %collective-permute-start.6 = (bf16[8,128,256]{2,1,0:T(8,128)(2,1)}, bf16[8,128,256]{2,1,0:T(8,128)(2,1)}, u32[]{:S(2)}, u32[]{:S(2)}) collective-permute-start(bf16[8,128,256]{2,1,0:T(8,128)(2,1)} %convert_element_type.139), channel_id=1, source_target_pairs={{0,1},{1,2},{2,3},{3,4},{4,5},{5,6},{6,7},{8,9},{9,10},{10,11},{11... | collective-permute-start | bytes 1572872 | tf_op jit(solution)/shard_map/ppermute | solution.py:20
  206.9 1.9 copy.258
  210.0 4.2 while.88
  210.7 1.3 convolution_add_fusion.23
  212.8 1.3 convolution_add_fusion.23
  214.2 6.3 %collective-permute-start.7 = (bf16[8,128,256]{2,1,0:T(8,128)(2,1)S(1)}, bf16[8,128,256]{2,1,0:T(8,128)(2,1)S(1)}, u32[]{:S(2)}, u32[]{:S(2)}) collective-permute-start(bf16[8,128,256]{2,1,0:T(8,128)(2,1)S(1)} %convert_element_type.141), channel_id=1, source_target_pairs={{0,1},{1,2},{2,3},{3,4},{4,5},{5,6},{6,7},{8,9},{9,10},{10,11},{11... | collective-permute-start | bytes 1572872 | tf_op jit(solution)/shard_map/ppermute | solution.py:20
  220.5 1.2 fusion.95
  222.9 1.9 fusion.70
  224.9 10.8 %while.89 = (s32[]{:T(128)}, f32[8,128,256]{2,1,0:T(8,128)S(1)}, f32[2,8,64,256]{3,2,1,0:T(8,128)}, f32[2,8]{1,0:T(2,128)S(1)}, f32[2,8,64,128]{3,2,1,0:T(8,128)...) while((s32[]{:T(128)}, f32[8,128,256]{2,1,0:T(8,128)S(1)}, ...), condition=%wide.region_20.21_spmd, body=%wide.region_19.20_spmd.sunk | while | flops 705429504 | bytes 19925256 | solution.py:85
  225.7 1.5 fusion.223
  229.0 1.3 convolution_add_fusion.24
  231.1 1.5 fusion.223
  234.4 1.3 convolution_add_fusion.24
  235.8 1.5 multiply_reduce_fusion.1
  237.6 1.4 copy.261
  239.6 1.3 copy.260
  241.0 5.8 %multiply_reduce_fusion = (f32[128]{0:T(128)S(1)}, f32[128,2048]{1,0:T(8,128)S(1)}) fusion(bf16[2048,2048]{1,0:T(8,128)(2,1)} %all-gather.6.cloned.1.call-done, f32[128,2048]{1,0:T(8,128)} %bitcast.348, f32[128,2048]{1,0:T(8,128)} %bitcast.347, bf16[1,128,2048]{2,1,0:T(8,128)(2,1)} %param.31, f32[2048]{0:T(1024)S(1)} %bitcast.360, ...), kind=kOutput, calls=%fused_computation.125 | convolution fusion | flops 1077673856 | bytes 12591616 | tf_op jit(solution)/shard_map/dot_general | solution.py:158
  249.9 1.4 copy.250
  252.6 6.2 %all-gather.10.cloned.1.call-done = bf16[2048,704]{0,1:T(8,128)(2,1)} async-done(((bf16[128,704]{0,1:T(8,128)(2,1)}), bf16[2048,704]{0,1:T(8,128)(2,1)}) %all-gather.10.cloned.1.call-update) | async-done | bytes 2883600 | tf_op jit(solution)/shard_map/all_gather | solution.py:169
  258.8 34.0 %all-gather.8.cloned.1.call-done = bf16[1024,2048]{1,0:T(8,128)(2,1)} async-done(((bf16[128,2048]{1,0:T(8,128)(2,1)}), bf16[1024,2048]{1,0:T(8,128)(2,1)}) %all-gather.8.cloned.1.call-update) | async-done | bytes 4194320 | tf_op jit(solution)/shard_map/all_gather | solution.py:173
  292.8 7.8 %fusion.114 = f32[1024,704]{0,1:T(8,128)} fusion(bf16[1024,2048]{1,0:T(8,128)(2,1)} %all-gather.8.cloned.1.call-done, bf16[2048,704]{0,1:T(8,128)(2,1)} %all-gather.10.cloned.1.call-done), kind=kOutput, calls=%fused_computation.195 | convolution fusion | flops 2952790016 | bytes 9961472 | tf_op jit(solution)/shard_map/dot_general | solution.py:174
  300.7 44.4 %all-gather.12.cloned.1.call-done = bf16[2048,704]{0,1:T(8,128)(2,1)} async-done(((bf16[128,704]{0,1:T(8,128)(2,1)}), bf16[2048,704]{0,1:T(8,128)(2,1)}) %all-gather.12.cloned.1.call-update) | async-done | bytes 2883600 | tf_op jit(solution)/shard_map/all_gather | solution.py:170
  345.1 51.8 %all-gather.14.cloned.1.call-done = bf16[704,2048]{1,0:T(8,128)(2,1)} async-done(((bf16[704,128]{1,0:T(8,128)(2,1)}), bf16[704,2048]{1,0:T(8,128)(2,1)}) %all-gather.14.cloned.1.call-update) | async-done | bytes 2883600 | tf_op jit(solution)/shard_map/all_gather | solution.py:172
  396.9 12.0 %convolution_convert_fusion.1 = bf16[1024,2048]{1,0:T(8,128)(2,1)} fusion(bf16[704,2048]{1,0:T(8,128)(2,1)} %all-gather.14.cloned.1.call-done, f32[1024,704]{0,1:T(8,128)} %fusion.114, bf16[1024,2048]{1,0:T(8,128)(2,1)} %all-gather.8.cloned.1.call-done, bf16[2048,704]{0,1:T(8,128)(2,1)} %all-gather.12.cloned.1.call-done), kind=kOutput, calls=%fused_computation.94 | convolution fusion | flops 5912002560 | bytes 17039360 | tf_op jit(solution)/shard_map/dot_general | solution.py:178
  409.5 21.5 %reduce-scatter.10.cloned.1.call-done = bf16[512,3]{1,0:T(8,128)(2,1)} async-done(((bf16[4096,3]{1,0:T(8,128)(2,1)}), bf16[512,3]{1,0:T(8,128)(2,1)}) %reduce-scatter.10.cloned.1.call-update) | async-done | bytes 3088
  431.0 1.6 copy.251
  432.6 31.0 %reduce-scatter.8.cloned.1.call-done = bf16[1,128,256]{2,1,0:T(8,128)(2,1)} async-done(((bf16[8,128,256]{2,1,0:T(8,128)(2,1)}), bf16[1,128,256]{2,1,0:T(8,128)(2,1)}) %reduce-scatter.8.cloned.1.call-update) | async-done | bytes 65552 | tf_op jit(solution)/shard_map/reduce_scatter | solution.py:144
  463.6 1.5 bitcast_convert_fusion
  465.1 37.8 %reduce-scatter.6.cloned.1.call-done = bf16[128,2048]{1,0:T(8,128)(2,1)} async-done(((bf16[1024,2048]{1,0:T(8,128)(2,1)}), bf16[128,2048]{1,0:T(8,128)(2,1)}) %reduce-scatter.6.cloned.1.call-update) | async-done | bytes 524304 | tf_op jit(solution)/shard_map/reduce_scatter | solution.py:177
  502.9 2.0 fusion.82
  (161 shorter events, 47.6 us)
Async XLA Ops:
  7.2 198.2 %copy-start = (f32[256]{0:T(256)S(1)}, f32[256]{0:T(256)}, u32[]{:S(2)}) copy-start(f32[256]{0:T(256)} %param.38) | copy-start | bytes 3076
  7.2 233.8 %all-gather.6.cloned.1.call-start = ((), (), s32[]{:S(2)}) async-start(), calls=%async_computation.3 | async-start | bytes 8454144 | tf_op jit(solution)/shard_map/all_gather | solution.py:160
  8.1 9.1 %collective-permute-start = (bf16[3,4096]{1,0:T(4,128)(2,1)S(1)}, bf16[3,4096]{1,0:T(4,128)(2,1)S(1)}, u32[]{:S(2)}, u32[]{:S(2)}) collective-permute-start(bf16[3,4096]{1,0:T(4,128)(2,1)S(1)} %slice_bitcast_fusion.2), channel_id=1, source_target_pairs={{0,1},{1,2},{2,3},{3,4},{4,5},{5,6},{6,7},{8,9},{9,10},{10,11},{11... | collective-permute-start | bytes 73736 | tf_op jit(solution)/shard_map/ppermute | solution.py:20
  9.4 249.4 %all-gather.10.cloned.1.call-start = ((), (), s32[]{:S(2)}) async-start(), calls=%async_computation.5 | async-start | bytes 3063808 | tf_op jit(solution)/shard_map/all_gather | solution.py:169
  20.6 1.7 copy-start.2
  23.9 83.9 %copy-start.9 = (f32[8,2,64,128]{3,0,2,1:T(8,128)}, f32[8,2,64,128]{3,0,2,1:T(8,128)S(1)}, u32[]{:S(2)}) copy-start(f32[8,2,64,128]{3,0,2,1:T(8,128)S(1)} %get-tuple-element.663) | copy-start | bytes 1572868
  23.9 85.7 %slice-start = ((f32[128,4096]{1,0:T(8,128)}), f32[128,2048]{1,0:T(8,128)S(1)}, s32[]{:S(2)}) async-start(f32[128,4096]{1,0:T(8,128)} %copy-done.2), calls=%async_computation.11 | async-start | bytes 2097152 | tf_op jit(solution)/shard_map/slice | solution.py:125
  116.8 6.6 %collective-permute-start.1 = (bf16[8,128,256]{2,1,0:T(8,128)(2,1)}, bf16[8,128,256]{2,1,0:T(8,128)(2,1)}, u32[]{:S(2)}, u32[]{:S(2)}) collective-permute-start(bf16[8,128,256]{2,1,0:T(8,128)(2,1)} %convert_element_type.129), channel_id=1, source_target_pairs={{0,1},{1,2},{2,3},{3,4},{4,5},{5,6},{6,7},{8,9},{9,10},{10,11},{11... | collective-permute-start | bytes 1572872 | tf_op jit(solution)/shard_map/ppermute | solution.py:20
  129.6 8.3 %collective-permute-start.2 = (bf16[8,128,256]{2,1,0:T(8,128)(2,1)}, bf16[8,128,256]{2,1,0:T(8,128)(2,1)}, u32[]{:S(2)}, u32[]{:S(2)}) collective-permute-start(bf16[8,128,256]{2,1,0:T(8,128)(2,1)} %convert_element_type.131), channel_id=1, source_target_pairs={{0,1},{1,2},{2,3},{3,4},{4,5},{5,6},{6,7},{8,9},{9,10},{10,11},{11... | collective-permute-start | bytes 1572872 | tf_op jit(solution)/shard_map/ppermute | solution.py:20
  144.2 10.8 %collective-permute-start.3 = (bf16[8,128,256]{2,1,0:T(8,128)(2,1)}, bf16[8,128,256]{2,1,0:T(8,128)(2,1)}, u32[]{:S(2)}, u32[]{:S(2)}) collective-permute-start(bf16[8,128,256]{2,1,0:T(8,128)(2,1)} %convert_element_type.133), channel_id=1, source_target_pairs={{0,1},{1,2},{2,3},{3,4},{4,5},{5,6},{6,7},{8,9},{9,10},{10,11},{11... | collective-permute-start | bytes 1572872 | tf_op jit(solution)/shard_map/ppermute | solution.py:20
  161.2 10.8 %collective-permute-start.4 = (bf16[8,128,256]{2,1,0:T(8,128)(2,1)}, bf16[8,128,256]{2,1,0:T(8,128)(2,1)}, u32[]{:S(2)}, u32[]{:S(2)}) collective-permute-start(bf16[8,128,256]{2,1,0:T(8,128)(2,1)} %convert_element_type.135), channel_id=1, source_target_pairs={{0,1},{1,2},{2,3},{3,4},{4,5},{5,6},{6,7},{8,9},{9,10},{10,11},{11... | collective-permute-start | bytes 1572872 | tf_op jit(solution)/shard_map/ppermute | solution.py:20
  178.3 10.8 %collective-permute-start.5 = (bf16[8,128,256]{2,1,0:T(8,128)(2,1)}, bf16[8,128,256]{2,1,0:T(8,128)(2,1)}, u32[]{:S(2)}, u32[]{:S(2)}) collective-permute-start(bf16[8,128,256]{2,1,0:T(8,128)(2,1)} %convert_element_type.137), channel_id=1, source_target_pairs={{0,1},{1,2},{2,3},{3,4},{4,5},{5,6},{6,7},{8,9},{9,10},{10,11},{11... | collective-permute-start | bytes 1572872 | tf_op jit(solution)/shard_map/ppermute | solution.py:20
  195.2 13.6 %collective-permute-start.6 = (bf16[8,128,256]{2,1,0:T(8,128)(2,1)}, bf16[8,128,256]{2,1,0:T(8,128)(2,1)}, u32[]{:S(2)}, u32[]{:S(2)}) collective-permute-start(bf16[8,128,256]{2,1,0:T(8,128)(2,1)} %convert_element_type.139), channel_id=1, source_target_pairs={{0,1},{1,2},{2,3},{3,4},{4,5},{5,6},{6,7},{8,9},{9,10},{10,11},{11... | collective-permute-start | bytes 1572872 | tf_op jit(solution)/shard_map/ppermute | solution.py:20
  205.0 87.8 %all-gather.8.cloned.1.call-start = ((), (), s32[]{:S(2)}) async-start(), calls=%async_computation.4 | async-start | bytes 4718592 | tf_op jit(solution)/shard_map/all_gather | solution.py:173
  214.2 7.6 %copy-start.4 = (f32[16,8,8,128]{3,2,1,0:T(8,128)S(1)}, f32[16,8,8,128]{3,2,1,0:T(8,128)}, u32[]{:S(2)}) copy-start(f32[16,8,8,128]{3,2,1,0:T(8,128)} %copy.258) | copy-start | bytes 1572868
  214.2 8.8 %copy-start.10 = (f32[8,2,64,128]{3,0,2,1:T(8,128)S(1)}, f32[8,2,64,128]{3,0,2,1:T(8,128)}, u32[]{:S(2)}) copy-start(f32[8,2,64,128]{3,0,2,1:T(8,128)} %copy-done.9) | copy-start | bytes 1572868
  214.2 10.6 %collective-permute-start.7 = (bf16[8,128,256]{2,1,0:T(8,128)(2,1)S(1)}, bf16[8,128,256]{2,1,0:T(8,128)(2,1)S(1)}, u32[]{:S(2)}, u32[]{:S(2)}) collective-permute-start(bf16[8,128,256]{2,1,0:T(8,128)(2,1)S(1)} %convert_element_type.141), channel_id=1, source_target_pairs={{0,1},{1,2},{2,3},{3,4},{4,5},{5,6},{6,7},{8,9},{9,10},{10,11},{11... | collective-permute-start | bytes 1572872 | tf_op jit(solution)/shard_map/ppermute | solution.py:20
  224.9 2.3 copy-start.3
  225.0 2.3 copy-start.6
  228.0 1.0 copy-start.7
  230.4 2.3 copy-start.3
  230.4 2.3 copy-start.6
  233.4 1.0 copy-start.7
  235.8 3.3 copy-start.8
  241.0 5.8 %copy-start.11 = (f32[2048]{0:T(1024)S(1)}, f32[2048]{0:T(1024)}, u32[]{:S(2)}) copy-start(f32[2048]{0:T(1024)} %param.40) | copy-start | bytes 24580
  241.0 8.6 %copy-start.5 = (bf16[1,128,4096]{2,1,0:T(8,128)(2,1)S(1)}, bf16[1,128,4096]{2,1,0:T(8,128)(2,1)}, u32[]{:S(2)}) copy-start(bf16[1,128,4096]{2,1,0:T(8,128)(2,1)} %param.30) | copy-start | bytes 3145732
  247.8 97.3 %all-gather.12.cloned.1.call-start = ((), (), s32[]{:S(2)}) async-start(), calls=%async_computation.6 | async-start | bytes 3063808 | tf_op jit(solution)/shard_map/all_gather | solution.py:170
  248.4 148.5 %all-gather.14.cloned.1.call-start = ((), (), s32[]{:S(2)}) async-start(), calls=%async_computation.7 | async-start | bytes 3063808 | tf_op jit(solution)/shard_map/all_gather | solution.py:172
  249.0 182.0 %reduce-scatter.10.cloned.1.call-start = ((), (), s32[]{:S(2)}) async-start(), calls=%async_computation.10 | async-start | bytes 1179648
  251.3 212.2 %reduce-scatter.8.cloned.1.call-start = ((), (), s32[]{:S(2)}) async-start(), calls=%async_computation.9 | async-start | bytes 589824 | tf_op jit(solution)/shard_map/reduce_scatter | solution.py:144
  252.3 250.5 %reduce-scatter.6.cloned.1.call-start = ((), (), s32[]{:S(2)}) async-start(), calls=%async_computation.8 | async-start | bytes 4718592 | tf_op jit(solution)/shard_map/reduce_scatter | solution.py:177
  408.9 96.0 %copy-start.1 = (f32[256]{0:T(256)S(1)}, f32[256]{0:T(256)}, u32[]{:S(2)}) copy-start(f32[256]{0:T(256)} %param.38) | copy-start | bytes 3076
Sparse Core Ops, SparseCore 0:
  11.0 74.0 all-gather.5
  205.1 53.6 all-gather.9
  261.1 31.6 all-gather.7
  294.8 50.2 all-gather.11
  347.0 49.8 all-gather.13
  399.2 31.8 reduce-scatter.9
  433.4 30.1 reduce-scatter.7
  466.0 36.8 reduce-scatter.5
where the time goes:
time: 521 us; the launch traced here: 512 us
  waiting for transfers between devices  233 us (45%)
  other arithmetic  114 us (22%)
  matrix products  71.7 us (14%)
  starting transfers between devices  60.5 us (12%)
  local copies, waits for them, and re-layouts  16.5 us (3%)
  between operations  15.4 us (3%)
    another operation x4, other arithmetic, block_tables(): lax.linalg.triangular_solve(identity + couple, identity, left_side=True,...  80.1 us
    ppermute x8, starting transfers between devices, shifted(): lax.ppermute(value, axis, [(source, source + steps) for source in range(i...  59.8 us
    all_gather x1, waiting for transfers between devices, local(): down_full = lax.all_gather(w_down, 'req', axis=1, tiled=True)  51.8 us
    all_gather x1, waiting for transfers between devices, local(): lax.all_gather(w_up, 'req', axis=0, tiled=True)  44.4 us
    reduce_scatter x1, waiting for transfers between devices, local(): lax.psum_scatter(jnp.dot(inner_units, down_full, preferred_element_type=j...  37.8 us
    all_gather x1, waiting for transfers between devices, local(): shard_rows = lax.all_gather(normed, 'seq', axis=0, tiled=True)  34 us
    reduce_scatter x1, waiting for transfers between devices, local(): lax.psum_scatter(state_term.astype(jnp.bfloat16), 'seq', scatter_dimensio...  31 us
    unnamed x9, waiting for transfers between devices  22.7 us
  transfers between devices with their start and end apart: 16, of which 12 were waited for; matrix products, arithmetic and copies ran while one was open for 39% of the time, Pallas kernels for 0%

commit v1 on v0

--- a/solution.py
+++ b/solution.py
@@ -12,6 +12,35 @@
 EPS_NORM = 1e-05
 EPS_UNIT = 1e-06
 HIGHEST = lax.Precision.HIGHEST
+
+
+def _number_heads(chunk, along_dim):
+    block_next = list(chunk.shape[1:])
+    block_next[along_dim] *= chunk.shape[0]
+    state_now = jnp.moveaxis(chunk, 0, along_dim).reshape(block_next)
+    return state_now
+
+
+def proceed_the_matrix(piece_in, dev_axis, pos_dim):
+    total_devices = lax.axis_size(dev_axis)
+    pages = tuple(((j0, (j0 + 1) % total_devices) for j0 in range(total_devices)))
+    column = tuple(((s, dev) for dev, s in pages))
+    part_now, n_now = ([], [])
+    dd = 0
+    while dd < total_devices - 1:
+        if dd % 2 == 0:
+            part_now.append(lax.ppermute(part_now[-1] if part_now else piece_in, dev_axis, pages))
+        else:
+            far_arr = lax.ppermute(n_now[-1] if n_now else piece_in, dev_axis, column)
+            n_now.append(far_arr)
+        dd += 1
+    latest = jnp.stack([*part_now[::-1], piece_in, *n_now], axis=0)
+    w2 = lax.axis_index(dev_axis)
+    lower = len(part_now)
+    e_next = w2 - lower
+    latest = latest[(jnp.arange(total_devices) - e_next) % total_devices]
+    val = _number_heads(latest, pos_dim)
+    return val
 
 
 def shifted(value, axis, steps):
@@ -167,7 +196,7 @@
     ).astype(jnp.bfloat16)
     gate_full, up_full = (
         lax.all_gather(w_gate, "req", axis=0, tiled=True),
-        lax.all_gather(w_up, "req", axis=0, tiled=True),
+        proceed_the_matrix(w_up, "req", 0),
     )
     down_full = lax.all_gather(w_down, "req", axis=1, tiled=True)
     shard_rows = lax.all_gather(normed, "seq", axis=0, tiled=True)

time: 521 us -> 472 us (0.906)
  waiting for transfers between devices: 233 us -> 119 us
  starting transfers between devices: 60.5 us -> 102 us
  local copies, waits for them, and re-layouts: 16.5 us -> 40 us
    all_gather x1, waiting for transfers between devices: 51.8 us -> 0.01 us  [local(): down_full = lax.all_gather(w_down, 'req', axis=1, tiled=True)]
    all_gather x1 -> x0, waiting for transfers between devices: 44.4 us -> none  [local(): lax.all_gather(w_up, 'req', axis=0, tiled=True)]
    ppermute x0 -> x15, starting transfers between devices: none -> 41.6 us  [the longest x7 40 us: proceed_the_matrix(): far_arr = lax.ppermute(n_now[-1] if n_now else piece_in, dev_axis, column)]
    all_gather x1, waiting for transfers between devices: 34 us -> 0.02 us  [local(): shard_rows = lax.all_gather(normed, 'seq', axis=0, tiled=True)]
    ppermute x0 -> x15, waiting for transfers between devices: none -> 33.5 us  [the longest x8 31.1 us: proceed_the_matrix(): lax.ppermute(part_now[-1] if part_now else piece_in, dev_axis, pages)]
    unnamed x32 -> x61, local copies, waits for them, and re-layouts: 9.73 us -> 28.2 us
    unnamed x9 -> x8, waiting for transfers between devices: 22.7 us -> 12.1 us
    all_gather x1, waiting for transfers between devices: 6.25 us -> 0.02 us  [local(): lax.all_gather(w_gate, 'req', axis=0, tiled=True)]
  transfers between devices with their start and end apart: 16 -> 30, of which waited for: 12 -> 21; matrix products, arithmetic and copies ran while one was open for 39% -> 48% of each run, Pallas kernels for 0% -> 0%
where the time goes in v1:
time: 472 us; the launch traced here: 464 us
  waiting for transfers between devices  119 us (25%)
  other arithmetic  114 us (24%)
  starting transfers between devices  102 us (22%)
  matrix products  71.9 us (15%)
  local copies, waits for them, and re-layouts  40 us (8%)
  between operations  15.7 us (3%)
    another operation x4, other arithmetic, block_tables(): lax.linalg.triangular_solve(identity + couple, identity, left_side=True,...  80.1 us
    ppermute x8, starting transfers between devices, shifted(): lax.ppermute(value, axis, [(source, source + steps) for source in range(i...  59.8 us
    ppermute x7, starting transfers between devices, proceed_the_matrix(): far_arr = lax.ppermute(n_now[-1] if n_now else piece_in, dev_axis, column)  40 us
    reduce_scatter x1, waiting for transfers between devices, local(): lax.psum_scatter(jnp.dot(inner_units, down_full, preferred_element_type=j...  37.7 us
    ppermute x8, waiting for transfers between devices, proceed_the_matrix(): lax.ppermute(part_now[-1] if part_now else piece_in, dev_axis, pages)  31.1 us
    reduce_scatter x1, waiting for transfers between devices, local(): lax.psum_scatter(state_term.astype(jnp.bfloat16), 'seq', scatter_dimensio...  30.8 us
    unnamed x61, local copies, waits for them, and re-layouts  28.2 us
    dot_general x16, matrix products, advance(): jnp.einsum('hck,hcx->hkx', keys_now, corrected, precision=HIGHEST)  21.1 us
  transfers between devices with their start and end apart: 30, of which 21 were waited for; matrix products, arithmetic and copies ran while one was open for 48% of the time, Pallas kernels for 0%

profile of v1, /device:TPU:0, one launch (start us, length us, event | category | flops | bytes accessed | tf_op | source)
XLA Modules:
  0.0 463.5 jit_solution(18137890377478582229)
XLA Ops:
  12.3 2.0 fusion.113
  17.4 3.5 divide_multiply_fusion
  20.8 1.4 multiply_bitcast_fusion
  24.1 1.8 fusion.77
  25.9 80.0 %custom-call.3 = f32[8,2,1,64,64]{3,4,2,1,0:T(8,128)} custom-call(f32[8,2,1,64,64]{4,3,2,1,0:T(8,128)} %fusion.77), custom_call_target="InvertDiagBlocksLowerTriangular" | custom-call | tf_op jit(solution)/shard_map/triangular_solve | solution.py:74
  105.9 2.0 fusion.92
  108.0 1.7 convolution_bitcast_fusion.2
  112.0 4.1 while.90
  117.0 6.0 %collective-permute-start.1 = (bf16[8,128,256]{2,1,0:T(8,128)(2,1)}, bf16[8,128,256]{2,1,0:T(8,128)(2,1)}, u32[]{:S(2)}, u32[]{:S(2)}) collective-permute-start(bf16[8,128,256]{2,1,0:T(8,128)(2,1)} %convert_element_type.129), channel_id=1, source_target_pairs={{0,1},{1,2},{2,3},{3,4},{4,5},{5,6},{6,7},{8,9},{9,10},{10,11},{11... | collective-permute-start | bytes 1572872 | tf_op jit(solution)/shard_map/ppermute | solution.py:49
  124.7 4.2 while.83
  129.7 7.3 %collective-permute-start.2 = (bf16[8,128,256]{2,1,0:T(8,128)(2,1)}, bf16[8,128,256]{2,1,0:T(8,128)(2,1)}, u32[]{:S(2)}, u32[]{:S(2)}) collective-permute-start(bf16[8,128,256]{2,1,0:T(8,128)(2,1)} %convert_element_type.131), channel_id=1, source_target_pairs={{0,1},{1,2},{2,3},{3,4},{4,5},{5,6},{6,7},{8,9},{9,10},{10,11},{11... | collective-permute-start | bytes 1572872 | tf_op jit(solution)/shard_map/ppermute | solution.py:49
  139.2 4.2 while.84
  144.2 9.7 %collective-permute-start.3 = (bf16[8,128,256]{2,1,0:T(8,128)(2,1)}, bf16[8,128,256]{2,1,0:T(8,128)(2,1)}, u32[]{:S(2)}, u32[]{:S(2)}) collective-permute-start(bf16[8,128,256]{2,1,0:T(8,128)(2,1)} %convert_element_type.133), channel_id=1, source_target_pairs={{0,1},{1,2},{2,3},{3,4},{4,5},{5,6},{6,7},{8,9},{9,10},{10,11},{11... | collective-permute-start | bytes 1572872 | tf_op jit(solution)/shard_map/ppermute | solution.py:49
  156.2 4.2 while.85
  161.2 9.7 %collective-permute-start.4 = (bf16[8,128,256]{2,1,0:T(8,128)(2,1)}, bf16[8,128,256]{2,1,0:T(8,128)(2,1)}, u32[]{:S(2)}, u32[]{:S(2)}) collective-permute-start(bf16[8,128,256]{2,1,0:T(8,128)(2,1)} %convert_element_type.135), channel_id=1, source_target_pairs={{0,1},{1,2},{2,3},{3,4},{4,5},{5,6},{6,7},{8,9},{9,10},{10,11},{11... | collective-permute-start | bytes 1572872 | tf_op jit(solution)/shard_map/ppermute | solution.py:49
  173.1 4.2 while.86
  178.2 9.8 %collective-permute-start.5 = (bf16[8,128,256]{2,1,0:T(8,128)(2,1)}, bf16[8,128,256]{2,1,0:T(8,128)(2,1)}, u32[]{:S(2)}, u32[]{:S(2)}) collective-permute-start(bf16[8,128,256]{2,1,0:T(8,128)(2,1)} %convert_element_type.137), channel_id=1, source_target_pairs={{0,1},{1,2},{2,3},{3,4},{4,5},{5,6},{6,7},{8,9},{9,10},{10,11},{11... | collective-permute-start | bytes 1572872 | tf_op jit(solution)/shard_map/ppermute | solution.py:49
  190.1 4.2 while.87
  195.1 9.8 %collective-permute-start.6 = (bf16[8,128,256]{2,1,0:T(8,128)(2,1)}, bf16[8,128,256]{2,1,0:T(8,128)(2,1)}, u32[]{:S(2)}, u32[]{:S(2)}) collective-permute-start(bf16[8,128,256]{2,1,0:T(8,128)(2,1)} %convert_element_type.139), channel_id=1, source_target_pairs={{0,1},{1,2},{2,3},{3,4},{4,5},{5,6},{6,7},{8,9},{9,10},{10,11},{11... | collective-permute-start | bytes 1572872 | tf_op jit(solution)/shard_map/ppermute | solution.py:49
  206.9 1.9 copy.263
  209.9 4.2 while.88
  214.2 6.3 %collective-permute-start.7 = (bf16[8,128,256]{2,1,0:T(8,128)(2,1)S(1)}, bf16[8,128,256]{2,1,0:T(8,128)(2,1)S(1)}, u32[]{:S(2)}, u32[]{:S(2)}) collective-permute-start(bf16[8,128,256]{2,1,0:T(8,128)(2,1)S(1)} %convert_element_type.141), channel_id=1, source_target_pairs={{0,1},{1,2},{2,3},{3,4},{4,5},{5,6},{6,7},{8,9},{9,10},{10,11},{11... | collective-permute-start | bytes 1572872 | tf_op jit(solution)/shard_map/ppermute | solution.py:49
  222.9 1.9 fusion.75
  224.9 10.8 %while.89 = (s32[]{:T(128)}, f32[8,128,256]{2,1,0:T(8,128)S(1)}, f32[2,8,64,256]{3,2,1,0:T(8,128)}, f32[2,8]{1,0:T(2,128)S(1)}, f32[2,8,64,128]{3,2,1,0:T(8,128)...) while((s32[]{:T(128)}, f32[8,128,256]{2,1,0:T(8,128)S(1)}, ...), condition=%wide.region_20.21_spmd, body=%wide.region_19.20_spmd.sunk | while | flops 705429504 | bytes 19925256 | solution.py:114
  225.7 1.5 fusion.232
  231.1 1.5 fusion.232
  235.7 1.5 multiply_reduce_fusion.1
  237.6 1.3 copy.266
  239.5 1.3 copy.265
  240.9 5.8 %multiply_reduce_fusion = (f32[128]{0:T(128)S(1)}, f32[128,2048]{1,0:T(8,128)S(1)}) fusion(bf16[2048,2048]{1,0:T(8,128)(2,1)} %all-gather.5.cloned.1.call-done, f32[128,2048]{1,0:T(8,128)} %bitcast.393, f32[128,2048]{1,0:T(8,128)} %bitcast.392, bf16[1,128,2048]{2,1,0:T(8,128)(2,1)} %param.31, f32[2048]{0:T(1024)S(1)} %bitcast.405, ...), kind=kOutput, calls=%fused_computation.129 | convolution fusion | flops 1077673856 | bytes 12591616 | tf_op jit(solution)/shard_map/dot_general | solution.py:187
  248.4 1.6 collective-permute-start.8
  249.9 8.1 %collective-permute-done.8 = bf16[128,704]{0,1:T(8,128)(2,1)S(1)} collective-permute-done((bf16[128,704]{0,1:T(8,128)(2,1)S(1)}, bf16[128,704]{0,1:T(8,128)(2,1)S(1)}, u32[]{:S(2)}, u32[]{:S(2)}) %collective-permute-start.8) | collective-permute-done | bytes 180256 | tf_op jit(solution)/shard_map/ppermute | solution.py:32
  258.1 5.5 %collective-permute-start.16 = (bf16[128,704]{0,1:T(8,128)(2,1)S(1)}, bf16[128,704]{0,1:T(8,128)(2,1)S(1)}, u32[]{:S(2)}, u32[]{:S(2)}) collective-permute-start(bf16[128,704]{0,1:T(8,128)(2,1)S(1)} %copy-done.11), channel_id=1, source_target_pairs={{8,0},{16,8},{24,16},{32,24},{40,32},{48,40},{56,48},{64,56},{72,6... | collective-permute-start | bytes 540680 | tf_op jit(solution)/shard_map/ppermute | solution.py:34
  263.6 3.3 collective-permute-done.9
  267.6 5.5 %collective-permute-start.17 = (bf16[128,704]{0,1:T(8,128)(2,1)S(1)}, bf16[128,704]{0,1:T(8,128)(2,1)}, u32[]{:S(2)}, u32[]{:S(2)}) collective-permute-start(bf16[128,704]{0,1:T(8,128)(2,1)S(1)} %collective-permute-done.16), channel_id=1, source_target_pairs={{8,0},{16,8},{24,16},{32,24},{40,32},{48,40},{56,48},{64,56},{72,6... | collective-permute-start | bytes 540680 | tf_op jit(solution)/shard_map/ppermute | solution.py:34
  273.1 2.6 collective-permute-done.10
  276.1 5.9 %collective-permute-start.18 = (bf16[128,704]{0,1:T(8,128)(2,1)}, bf16[128,704]{0,1:T(8,128)(2,1)}, u32[]{:S(2)}, u32[]{:S(2)}) collective-permute-start(bf16[128,704]{0,1:T(8,128)(2,1)} %collective-permute-done.17), channel_id=1, source_target_pairs={{8,0},{16,8},{24,16},{32,24},{40,32},{48,40},{56,48},{64,56},{72,6... | collective-permute-start | bytes 540680 | tf_op jit(solution)/shard_map/ppermute | solution.py:34
  282.0 3.0 collective-permute-done.11
  286.0 5.8 %collective-permute-start.19 = (bf16[128,704]{0,1:T(8,128)(2,1)}, bf16[128,704]{0,1:T(8,128)(2,1)}, u32[]{:S(2)}, u32[]{:S(2)}) collective-permute-start(bf16[128,704]{0,1:T(8,128)(2,1)} %collective-permute-done.18), channel_id=1, source_target_pairs={{8,0},{16,8},{24,16},{32,24},{40,32},{48,40},{56,48},{64,56},{72,6... | collective-permute-start | bytes 540680 | tf_op jit(solution)/shard_map/ppermute | solution.py:34
  291.8 3.9 collective-permute-done.12
  297.0 5.8 %collective-permute-start.20 = (bf16[128,704]{0,1:T(8,128)(2,1)}, bf16[128,704]{0,1:T(8,128)(2,1)}, u32[]{:S(2)}, u32[]{:S(2)}) collective-permute-start(bf16[128,704]{0,1:T(8,128)(2,1)} %collective-permute-done.19), channel_id=1, source_target_pairs={{8,0},{16,8},{24,16},{32,24},{40,32},{48,40},{56,48},{64,56},{72,6... | collective-permute-start | bytes 540680 | tf_op jit(solution)/shard_map/ppermute | solution.py:34
  302.8 3.2 collective-permute-done.13
  306.3 1.4 copy.254
  308.2 5.8 %collective-permute-start.21 = (bf16[128,704]{0,1:T(8,128)(2,1)}, bf16[128,704]{0,1:T(8,128)(2,1)S(1)}, u32[]{:S(2)}, u32[]{:S(2)}) collective-permute-start(bf16[128,704]{0,1:T(8,128)(2,1)} %collective-permute-done.20), channel_id=1, source_target_pairs={{8,0},{16,8},{24,16},{32,24},{40,32},{48,40},{56,48},{64,56},{72,6... | collective-permute-start | bytes 540680 | tf_op jit(solution)/shard_map/ppermute | solution.py:34
  314.0 3.7 collective-permute-done.14
  317.8 5.7 %collective-permute-start.22 = (bf16[128,704]{0,1:T(8,128)(2,1)S(1)}, bf16[128,704]{0,1:T(8,128)(2,1)S(1)}, u32[]{:S(2)}, u32[]{:S(2)}) collective-permute-start(bf16[128,704]{0,1:T(8,128)(2,1)S(1)} %collective-permute-done.21), channel_id=1, source_target_pairs={{8,0},{16,8},{24,16},{32,24},{40,32},{48,40},{56,48},{64,56},{72,6... | collective-permute-start | bytes 540680 | tf_op jit(solution)/shard_map/ppermute | solution.py:34
  323.5 3.2 collective-permute-done.15
  327.4 1.6 bitcast_dynamic-update-slice_fusion.14
  329.0 1.6 bitcast_dynamic-update-slice_fusion.13
  330.7 1.6 bitcast_dynamic-update-slice_fusion.12
  332.3 1.6 bitcast_dynamic-update-slice_fusion.11
  337.3 1.6 bitcast_dynamic-update-slice_fusion.5
  338.9 1.6 bitcast_dynamic-update-slice_fusion.4
  340.5 1.6 bitcast_dynamic-update-slice_fusion.3
  342.1 1.6 bitcast_dynamic-update-slice_fusion.2
  345.1 4.3 gather_fusion
  350.7 7.8 %fusion.123 = f32[1024,704]{0,1:T(8,128)} fusion(bf16[1024,2048]{1,0:T(8,128)(2,1)} %all-gather.7.cloned.1.call-done, bf16[2048,704]{0,1:T(8,128)(2,1)} %all-gather.9.cloned.1.call-done), kind=kOutput, calls=%fused_computation.222 | convolution fusion | flops 2952790016 | bytes 9961472 | tf_op jit(solution)/shard_map/dot_general | solution.py:203
  358.5 12.1 %convolution_convert_fusion.1 = bf16[1024,2048]{1,0:T(8,128)(2,1)} fusion(bf16[704,2048]{1,0:T(8,128)(2,1)} %all-gather.11.cloned.1.call-done, f32[1024,704]{0,1:T(8,128)} %fusion.123, bf16[1024,2048]{1,0:T(8,128)(2,1)} %all-gather.7.cloned.1.call-done, bf16[16,128,704]{1,2,0:T(8,128)(2,1)} %gather_fusion), kind=kOutput, calls=%fused_computation.95 | convolution fusion | flops 5912002560 | bytes 17039360 | tf_op jit(solution)/shard_map/dot_general | solution.py:207
  371.3 11.5 %reduce-scatter.10.cloned.1.call-done = bf16[512,3]{1,0:T(8,128)(2,1)} async-done(((bf16[4096,3]{1,0:T(8,128)(2,1)}), bf16[512,3]{1,0:T(8,128)(2,1)}) %reduce-scatter.10.cloned.1.call-update) | async-done | bytes 3088
  382.8 1.6 copy.255
  384.4 30.8 %reduce-scatter.8.cloned.1.call-done = bf16[1,128,256]{2,1,0:T(8,128)(2,1)} async-done(((bf16[8,128,256]{2,1,0:T(8,128)(2,1)}), bf16[1,128,256]{2,1,0:T(8,128)(2,1)}) %reduce-scatter.8.cloned.1.call-update) | async-done | bytes 65552 | tf_op jit(solution)/shard_map/reduce_scatter | solution.py:173
  415.2 1.5 bitcast_convert_fusion
  416.7 37.7 %reduce-scatter.6.cloned.1.call-done = bf16[128,2048]{1,0:T(8,128)(2,1)} async-done(((bf16[1024,2048]{1,0:T(8,128)(2,1)}), bf16[128,2048]{1,0:T(8,128)(2,1)}) %reduce-scatter.6.cloned.1.call-update) | async-done | bytes 524304 | tf_op jit(solution)/shard_map/reduce_scatter | solution.py:206
  454.4 2.0 fusion.89
  (221 shorter events, 83.1 us)
Async XLA Ops:
  7.2 198.1 %copy-start = (f32[256]{0:T(256)S(1)}, f32[256]{0:T(256)}, u32[]{:S(2)}) copy-start(f32[256]{0:T(256)} %param.38) | copy-start | bytes 3076
  7.2 233.7 %all-gather.5.cloned.1.call-start = ((), (), s32[]{:S(2)}) async-start(), calls=%async_computation.3 | async-start | bytes 8454144 | tf_op jit(solution)/shard_map/all_gather | solution.py:189
  8.1 9.3 %collective-permute-start = (bf16[3,4096]{1,0:T(4,128)(2,1)S(1)}, bf16[3,4096]{1,0:T(4,128)(2,1)S(1)}, u32[]{:S(2)}, u32[]{:S(2)}) collective-permute-start(bf16[3,4096]{1,0:T(4,128)(2,1)S(1)} %slice_bitcast_fusion.2), channel_id=1, source_target_pairs={{0,1},{1,2},{2,3},{3,4},{4,5},{5,6},{6,7},{8,9},{9,10},{10,11},{11... | collective-permute-start | bytes 73736 | tf_op jit(solution)/shard_map/ppermute | solution.py:49
  9.4 341.2 %all-gather.9.cloned.1.call-start = ((), (), s32[]{:S(2)}) async-start(), calls=%async_computation.5 | async-start | bytes 3063808 | tf_op jit(solution)/shard_map/all_gather | solution.py:198
  20.8 1.7 copy-start.2
  24.1 83.9 %copy-start.9 = (f32[8,2,64,128]{3,0,2,1:T(8,128)}, f32[8,2,64,128]{3,0,2,1:T(8,128)S(1)}, u32[]{:S(2)}) copy-start(f32[8,2,64,128]{3,0,2,1:T(8,128)S(1)} %get-tuple-element.663) | copy-start | bytes 1572868
  24.1 85.7 %slice-start = ((f32[128,4096]{1,0:T(8,128)}), f32[128,2048]{1,0:T(8,128)S(1)}, s32[]{:S(2)}) async-start(f32[128,4096]{1,0:T(8,128)} %copy-done.2), calls=%async_computation.10 | async-start | bytes 2097152 | tf_op jit(solution)/shard_map/slice | solution.py:154
  117.0 6.5 %collective-permute-start.1 = (bf16[8,128,256]{2,1,0:T(8,128)(2,1)}, bf16[8,128,256]{2,1,0:T(8,128)(2,1)}, u32[]{:S(2)}, u32[]{:S(2)}) collective-permute-start(bf16[8,128,256]{2,1,0:T(8,128)(2,1)} %convert_element_type.129), channel_id=1, source_target_pairs={{0,1},{1,2},{2,3},{3,4},{4,5},{5,6},{6,7},{8,9},{9,10},{10,11},{11... | collective-permute-start | bytes 1572872 | tf_op jit(solution)/shard_map/ppermute | solution.py:49
  129.7 8.3 %collective-permute-start.2 = (bf16[8,128,256]{2,1,0:T(8,128)(2,1)}, bf16[8,128,256]{2,1,0:T(8,128)(2,1)}, u32[]{:S(2)}, u32[]{:S(2)}) collective-permute-start(bf16[8,128,256]{2,1,0:T(8,128)(2,1)} %convert_element_type.131), channel_id=1, source_target_pairs={{0,1},{1,2},{2,3},{3,4},{4,5},{5,6},{6,7},{8,9},{9,10},{10,11},{11... | collective-permute-start | bytes 1572872 | tf_op jit(solution)/shard_map/ppermute | solution.py:49
  144.2 10.8 %collective-permute-start.3 = (bf16[8,128,256]{2,1,0:T(8,128)(2,1)}, bf16[8,128,256]{2,1,0:T(8,128)(2,1)}, u32[]{:S(2)}, u32[]{:S(2)}) collective-permute-start(bf16[8,128,256]{2,1,0:T(8,128)(2,1)} %convert_element_type.133), channel_id=1, source_target_pairs={{0,1},{1,2},{2,3},{3,4},{4,5},{5,6},{6,7},{8,9},{9,10},{10,11},{11... | collective-permute-start | bytes 1572872 | tf_op jit(solution)/shard_map/ppermute | solution.py:49
  161.2 10.8 %collective-permute-start.4 = (bf16[8,128,256]{2,1,0:T(8,128)(2,1)}, bf16[8,128,256]{2,1,0:T(8,128)(2,1)}, u32[]{:S(2)}, u32[]{:S(2)}) collective-permute-start(bf16[8,128,256]{2,1,0:T(8,128)(2,1)} %convert_element_type.135), channel_id=1, source_target_pairs={{0,1},{1,2},{2,3},{3,4},{4,5},{5,6},{6,7},{8,9},{9,10},{10,11},{11... | collective-permute-start | bytes 1572872 | tf_op jit(solution)/shard_map/ppermute | solution.py:49
  178.2 10.8 %collective-permute-start.5 = (bf16[8,128,256]{2,1,0:T(8,128)(2,1)}, bf16[8,128,256]{2,1,0:T(8,128)(2,1)}, u32[]{:S(2)}, u32[]{:S(2)}) collective-permute-start(bf16[8,128,256]{2,1,0:T(8,128)(2,1)} %convert_element_type.137), channel_id=1, source_target_pairs={{0,1},{1,2},{2,3},{3,4},{4,5},{5,6},{6,7},{8,9},{9,10},{10,11},{11... | collective-permute-start | bytes 1572872 | tf_op jit(solution)/shard_map/ppermute | solution.py:49
  195.1 13.6 %collective-permute-start.6 = (bf16[8,128,256]{2,1,0:T(8,128)(2,1)}, bf16[8,128,256]{2,1,0:T(8,128)(2,1)}, u32[]{:S(2)}, u32[]{:S(2)}) collective-permute-start(bf16[8,128,256]{2,1,0:T(8,128)(2,1)} %convert_element_type.139), channel_id=1, source_target_pairs={{0,1},{1,2},{2,3},{3,4},{4,5},{5,6},{6,7},{8,9},{9,10},{10,11},{11... | collective-permute-start | bytes 1572872 | tf_op jit(solution)/shard_map/ppermute | solution.py:49
  204.9 145.7 %all-gather.7.cloned.1.call-start = ((), (), s32[]{:S(2)}) async-start(), calls=%async_computation.4 | async-start | bytes 4718592 | tf_op jit(solution)/shard_map/all_gather | solution.py:202
  214.1 7.6 %copy-start.4 = (f32[16,8,8,128]{3,2,1,0:T(8,128)S(1)}, f32[16,8,8,128]{3,2,1,0:T(8,128)}, u32[]{:S(2)}) copy-start(f32[16,8,8,128]{3,2,1,0:T(8,128)} %copy.263) | copy-start | bytes 1572868
  214.1 8.8 %copy-start.10 = (f32[8,2,64,128]{3,0,2,1:T(8,128)S(1)}, f32[8,2,64,128]{3,0,2,1:T(8,128)}, u32[]{:S(2)}) copy-start(f32[8,2,64,128]{3,0,2,1:T(8,128)} %copy-done.9) | copy-start | bytes 1572868
  214.2 10.6 %collective-permute-start.7 = (bf16[8,128,256]{2,1,0:T(8,128)(2,1)S(1)}, bf16[8,128,256]{2,1,0:T(8,128)(2,1)S(1)}, u32[]{:S(2)}, u32[]{:S(2)}) collective-permute-start(bf16[8,128,256]{2,1,0:T(8,128)(2,1)S(1)} %convert_element_type.141), channel_id=1, source_target_pairs={{0,1},{1,2},{2,3},{3,4},{4,5},{5,6},{6,7},{8,9},{9,10},{10,11},{11... | collective-permute-start | bytes 1572872 | tf_op jit(solution)/shard_map/ppermute | solution.py:49
  224.9 2.3 copy-start.3
  224.9 2.3 copy-start.6
  228.0 1.0 copy-start.7
  230.3 2.3 copy-start.3
  230.3 2.3 copy-start.6
  233.4 1.0 copy-start.7
  235.7 3.2 copy-start.8
  240.9 5.9 %copy-start.18 = (f32[2048]{0:T(1024)S(1)}, f32[2048]{0:T(1024)}, u32[]{:S(2)}) copy-start(f32[2048]{0:T(1024)} %param.40) | copy-start | bytes 24580
  240.9 7.5 %copy-start.11 = (bf16[128,704]{0,1:T(8,128)(2,1)S(1)}, bf16[128,704]{0,1:T(8,128)(2,1)}, u32[]{:S(2)}) copy-start(bf16[128,704]{0,1:T(8,128)(2,1)} %param.42) | copy-start | bytes 540676
  240.9 65.1 %copy-start.5 = (bf16[1,128,4096]{2,1,0:T(8,128)(2,1)S(1)}, bf16[1,128,4096]{2,1,0:T(8,128)(2,1)}, u32[]{:S(2)}) copy-start(bf16[1,128,4096]{2,1,0:T(8,128)(2,1)} %param.30) | copy-start | bytes 3145732
  247.7 110.8 %all-gather.11.cloned.1.call-start = ((), (), s32[]{:S(2)}) async-start(), calls=%async_computation.6 | async-start | bytes 3063808 | tf_op jit(solution)/shard_map/all_gather | solution.py:201
  248.3 134.5 %reduce-scatter.10.cloned.1.call-start = ((), (), s32[]{:S(2)}) async-start(), calls=%async_computation.9 | async-start | bytes 1179648
  248.4 9.7 %collective-permute-start.8 = (bf16[128,704]{0,1:T(8,128)(2,1)S(1)}, bf16[128,704]{0,1:T(8,128)(2,1)S(1)}, u32[]{:S(2)}, u32[]{:S(2)}) collective-permute-start(bf16[128,704]{0,1:T(8,128)(2,1)S(1)} %copy-done.11), channel_id=1, source_target_pairs={{0,8},{8,16},{16,24},{24,32},{32,40},{40,48},{48,56},{56,64},{64,7... | collective-permute-start | bytes 540680 | tf_op jit(solution)/shard_map/ppermute | solution.py:32
  258.1 8.8 %collective-permute-start.9 = (bf16[128,704]{0,1:T(8,128)(2,1)S(1)}, bf16[128,704]{0,1:T(8,128)(2,1)S(1)}, u32[]{:S(2)}, u32[]{:S(2)}) collective-permute-start(bf16[128,704]{0,1:T(8,128)(2,1)S(1)} %collective-permute-done.8), channel_id=1, source_target_pairs={{0,8},{8,16},{16,24},{24,32},{32,40},{40,48},{48,56},{56,64},{64,7... | collective-permute-start | bytes 540680 | tf_op jit(solution)/shard_map/ppermute | solution.py:32
  258.1 8.8 %collective-permute-start.16 = (bf16[128,704]{0,1:T(8,128)(2,1)S(1)}, bf16[128,704]{0,1:T(8,128)(2,1)S(1)}, u32[]{:S(2)}, u32[]{:S(2)}) collective-permute-start(bf16[128,704]{0,1:T(8,128)(2,1)S(1)} %copy-done.11), channel_id=1, source_target_pairs={{8,0},{16,8},{24,16},{32,24},{40,32},{48,40},{56,48},{64,56},{72,6... | collective-permute-start | bytes 540680 | tf_op jit(solution)/shard_map/ppermute | solution.py:34
  266.9 9.2 %copy-start.14 = (bf16[128,704]{0,1:T(8,128)(2,1)}, bf16[128,704]{0,1:T(8,128)(2,1)S(1)}, u32[]{:S(2)}) copy-start(bf16[128,704]{0,1:T(8,128)(2,1)S(1)} %collective-permute-done.9) | copy-start | bytes 540676
  266.9 8.8 %collective-permute-start.10 = (bf16[128,704]{0,1:T(8,128)(2,1)S(1)}, bf16[128,704]{0,1:T(8,128)(2,1)S(1)}, u32[]{:S(2)}, u32[]{:S(2)}) collective-permute-start(bf16[128,704]{0,1:T(8,128)(2,1)S(1)} %collective-permute-done.9), channel_id=1, source_target_pairs={{0,8},{8,16},{16,24},{24,32},{32,40},{40,48},{48,56},{56,64},{64,7... | collective-permute-start | bytes 540680 | tf_op jit(solution)/shard_map/ppermute | solution.py:32
  266.9 0.7 copy-start.12
  267.6 8.5 %collective-permute-start.17 = (bf16[128,704]{0,1:T(8,128)(2,1)S(1)}, bf16[128,704]{0,1:T(8,128)(2,1)}, u32[]{:S(2)}, u32[]{:S(2)}) collective-permute-start(bf16[128,704]{0,1:T(8,128)(2,1)S(1)} %collective-permute-done.16), channel_id=1, source_target_pairs={{8,0},{16,8},{24,16},{32,24},{40,32},{48,40},{56,48},{64,56},{72,6... | collective-permute-start | bytes 540680 | tf_op jit(solution)/shard_map/ppermute | solution.py:34
  275.7 6.3 %copy-start.16 = (bf16[128,704]{0,1:T(8,128)(2,1)}, bf16[128,704]{0,1:T(8,128)(2,1)S(1)}, u32[]{:S(2)}) copy-start(bf16[128,704]{0,1:T(8,128)(2,1)S(1)} %collective-permute-done.10) | copy-start | bytes 540676
  275.7 9.3 %collective-permute-start.11 = (bf16[128,704]{0,1:T(8,128)(2,1)S(1)}, bf16[128,704]{0,1:T(8,128)(2,1)}, u32[]{:S(2)}, u32[]{:S(2)}) collective-permute-start(bf16[128,704]{0,1:T(8,128)(2,1)S(1)} %collective-permute-done.10), channel_id=1, source_target_pairs={{0,8},{8,16},{16,24},{24,32},{32,40},{40,48},{48,56},{56,64},{64,7... | collective-permute-start | bytes 540680 | tf_op jit(solution)/shard_map/ppermute | solution.py:32
  276.1 9.9 %collective-permute-start.18 = (bf16[128,704]{0,1:T(8,128)(2,1)}, bf16[128,704]{0,1:T(8,128)(2,1)}, u32[]{:S(2)}, u32[]{:S(2)}) collective-permute-start(bf16[128,704]{0,1:T(8,128)(2,1)} %collective-permute-done.17), channel_id=1, source_target_pairs={{8,0},{16,8},{24,16},{32,24},{40,32},{48,40},{56,48},{64,56},{72,6... | collective-permute-start | bytes 540680 | tf_op jit(solution)/shard_map/ppermute | solution.py:34
  285.0 10.7 %collective-permute-start.12 = (bf16[128,704]{0,1:T(8,128)(2,1)}, bf16[128,704]{0,1:T(8,128)(2,1)}, u32[]{:S(2)}, u32[]{:S(2)}) collective-permute-start(bf16[128,704]{0,1:T(8,128)(2,1)} %collective-permute-done.11), channel_id=1, source_target_pairs={{0,8},{8,16},{16,24},{24,32},{32,40},{40,48},{48,56},{56,64},{64,7... | collective-permute-start | bytes 540680 | tf_op jit(solution)/shard_map/ppermute | solution.py:32
  286.0 11.0 %collective-permute-start.19 = (bf16[128,704]{0,1:T(8,128)(2,1)}, bf16[128,704]{0,1:T(8,128)(2,1)}, u32[]{:S(2)}, u32[]{:S(2)}) collective-permute-start(bf16[128,704]{0,1:T(8,128)(2,1)} %collective-permute-done.18), channel_id=1, source_target_pairs={{8,0},{16,8},{24,16},{32,24},{40,32},{48,40},{56,48},{64,56},{72,6... | collective-permute-start | bytes 540680 | tf_op jit(solution)/shard_map/ppermute | solution.py:34
  295.7 10.3 %collective-permute-start.13 = (bf16[128,704]{0,1:T(8,128)(2,1)}, bf16[128,704]{0,1:T(8,128)(2,1)}, u32[]{:S(2)}, u32[]{:S(2)}) collective-permute-start(bf16[128,704]{0,1:T(8,128)(2,1)} %collective-permute-done.12), channel_id=1, source_target_pairs={{0,8},{8,16},{16,24},{24,32},{32,40},{40,48},{48,56},{56,64},{64,7... | collective-permute-start | bytes 540680 | tf_op jit(solution)/shard_map/ppermute | solution.py:32
  297.0 11.2 %collective-permute-start.20 = (bf16[128,704]{0,1:T(8,128)(2,1)}, bf16[128,704]{0,1:T(8,128)(2,1)}, u32[]{:S(2)}, u32[]{:S(2)}) collective-permute-start(bf16[128,704]{0,1:T(8,128)(2,1)} %collective-permute-done.19), channel_id=1, source_target_pairs={{8,0},{16,8},{24,16},{32,24},{40,32},{48,40},{56,48},{64,56},{72,6... | collective-permute-start | bytes 540680 | tf_op jit(solution)/shard_map/ppermute | solution.py:34
  306.0 11.7 %collective-permute-start.14 = (bf16[128,704]{0,1:T(8,128)(2,1)}, bf16[128,704]{0,1:T(8,128)(2,1)}, u32[]{:S(2)}, u32[]{:S(2)}) collective-permute-start(bf16[128,704]{0,1:T(8,128)(2,1)} %collective-permute-done.13), channel_id=1, source_target_pairs={{0,8},{8,16},{16,24},{24,32},{32,40},{40,48},{48,56},{56,64},{64,7... | collective-permute-start | bytes 540680 | tf_op jit(solution)/shard_map/ppermute | solution.py:32
  306.3 27.6 %copy-start.17 = (bf16[128,704]{0,1:T(8,128)(2,1)S(1)}, bf16[128,704]{0,1:T(8,128)(2,1)}, u32[]{:S(2)}) copy-start(bf16[128,704]{0,1:T(8,128)(2,1)} %copy-done.16) | copy-start | bytes 540676
  306.3 28.3 %copy-start.15 = (bf16[128,704]{0,1:T(8,128)(2,1)S(1)}, bf16[128,704]{0,1:T(8,128)(2,1)}, u32[]{:S(2)}) copy-start(bf16[128,704]{0,1:T(8,128)(2,1)} %copy-done.14) | copy-start | bytes 540676
  306.3 30.3 %copy-start.13 = (bf16[128,704]{0,1:T(8,128)(2,1)S(1)}, bf16[128,704]{0,1:T(8,128)(2,1)}, u32[]{:S(2)}) copy-start(bf16[128,704]{0,1:T(8,128)(2,1)} %copy-done.12) | copy-start | bytes 540676
  307.7 107.5 %reduce-scatter.8.cloned.1.call-start = ((), (), s32[]{:S(2)}) async-start(), calls=%async_computation.8 | async-start | bytes 589824 | tf_op jit(solution)/shard_map/reduce_scatter | solution.py:173
  308.2 9.6 %collective-permute-start.21 = (bf16[128,704]{0,1:T(8,128)(2,1)}, bf16[128,704]{0,1:T(8,128)(2,1)S(1)}, u32[]{:S(2)}, u32[]{:S(2)}) collective-permute-start(bf16[128,704]{0,1:T(8,128)(2,1)} %collective-permute-done.20), channel_id=1, source_target_pairs={{8,0},{16,8},{24,16},{32,24},{40,32},{48,40},{56,48},{64,56},{72,6... | collective-permute-start | bytes 540680 | tf_op jit(solution)/shard_map/ppermute | solution.py:34
  317.7 9.0 %collective-permute-start.15 = (bf16[128,704]{0,1:T(8,128)(2,1)}, bf16[128,704]{0,1:T(8,128)(2,1)S(1)}, u32[]{:S(2)}, u32[]{:S(2)}) collective-permute-start(bf16[128,704]{0,1:T(8,128)(2,1)} %collective-permute-done.14), channel_id=1, source_target_pairs={{0,8},{8,16},{16,24},{24,32},{32,40},{40,48},{48,56},{56,64},{64,7... | collective-permute-start | bytes 540680 | tf_op jit(solution)/shard_map/ppermute | solution.py:32
  317.8 26.7 %collective-permute-start.22 = (bf16[128,704]{0,1:T(8,128)(2,1)S(1)}, bf16[128,704]{0,1:T(8,128)(2,1)S(1)}, u32[]{:S(2)}, u32[]{:S(2)}) collective-permute-start(bf16[128,704]{0,1:T(8,128)(2,1)S(1)} %collective-permute-done.21), channel_id=1, source_target_pairs={{8,0},{16,8},{24,16},{32,24},{40,32},{48,40},{56,48},{64,56},{72,6... | collective-permute-start | bytes 540680 | tf_op jit(solution)/shard_map/ppermute | solution.py:34
  350.3 104.1 %reduce-scatter.6.cloned.1.call-start = ((), (), s32[]{:S(2)}) async-start(), calls=%async_computation.7 | async-start | bytes 4718592 | tf_op jit(solution)/shard_map/reduce_scatter | solution.py:206
  370.6 85.8 %copy-start.1 = (f32[256]{0:T(256)S(1)}, f32[256]{0:T(256)}, u32[]{:S(2)}) copy-start(f32[256]{0:T(256)} %param.38) | copy-start | bytes 3076
Sparse Core Ops, SparseCore 0:
  11.0 74.2 all-gather.4
  205.1 56.5 all-gather.8
  264.0 29.6 all-gather.6
  295.7 51.7 all-gather.10
  349.7 33.0 reduce-scatter.9
  385.0 30.1 reduce-scatter.7
  417.6 36.7 reduce-scatter.5
